TPU v7x, 512 devices: a whole 4x4x16 slice. The times are simulated.
512 devices in a mesh: section: 8 (over z_lo), dp: 16 (over x, z_hi, core), tensor: 4 (over y).
Axes of the slice: x: 4, y: 4, z: 16 (z_hi: 2, z_lo: 8; z = z_hi * 8 + z_lo), core: 2. Of those that a mesh axis runs over, the one named last changes fastest.
Arguments:
- norm_in: bfloat16 [8, 2048, 8192], P('section', 'dp', 'tensor'), may hold values from -20 to 20
- query_grad: bfloat16 [8, 2048, 4096], P('section', 'dp', 'tensor'), may hold values from -20 to 20
- attn_out: bfloat16 [8, 2048, 4096], P('section', 'dp', 'tensor'), may hold values from -20 to 20
- handed: bfloat16 [8, 2048, 8192], P('section', 'dp', 'tensor'), may hold values from -20 to 20
- sketch_q: bfloat16 [8, 64, 4096], P('section', None, 'tensor'), may hold values from -6 to 6
- sketch_o: bfloat16 [8, 64, 8192], P('section', None, 'tensor'), may hold values from -6 to 6
Outputs:
- lora_b_q: bfloat16 [8, 64, 8192], P('section', None, 'tensor')
- lora_a_q: float32 [8, 64, 4096], P('section', None, 'tensor')
- lora_b_o: bfloat16 [8, 64, 4096], P('section', None, 'tensor')
- lora_a_o: float32 [8, 64, 8192], P('section', None, 'tensor')
All inputs are finite; a program needn't handle non-finite values.
Results may differ from a plain program's by a relative error of at most 0.03.
Values may be sent and summed in bfloat16 or wider, within the bound.
A program may use at most 64 MiB of HBM per device.

v0:
```python
import jax
import jax.numpy as jnp
from jax import lax
from jax.sharding import PartitionSpec as P

D = 8192
HQ = 4096
RANK = 64
POWER = 2


precise = lax.Precision.HIGHEST


def from_behind(value, axis, steps):
    count = lax.axis_size(axis)
    pairs = [(source, (source + steps) % count) for source in range(count)]
    return lax.ppermute(value, axis, pairs)


def gram_of(row_block):
    return jnp.dot(row_block, row_block.T, precision=precise, preferred_element_type=jnp.float32)


def solve_rows(gram_rows, row_block):
    low_factor = jnp.linalg.cholesky(gram_rows)
    solved = lax.linalg.triangular_solve(low_factor, row_block, left_side=True, lower=True)
    return solved.astype(jnp.bfloat16)


def tokens_of(sketches, matrices):
    first_part = jnp.einsum(
        "km,tm->kt", sketches[0], matrices[0], preferred_element_type=jnp.float32
    )
    second_part = jnp.einsum(
        "km,tm->kt", sketches[1], matrices[1], preferred_element_type=jnp.float32
    )
    total_a, total_b = (
        lax.psum(first_part.astype(jnp.bfloat16), "tensor").astype(jnp.float32),
        lax.psum(second_part.astype(jnp.bfloat16), "tensor").astype(jnp.float32),
    )
    return (total_a.astype(jnp.bfloat16), total_b.astype(jnp.bfloat16))


def partials(token_rows, matrices):
    part_a = jnp.dot(token_rows[0], matrices[0], preferred_element_type=jnp.float32)
    part_b = jnp.dot(token_rows[1], matrices[1], preferred_element_type=jnp.float32)
    return (part_a, part_b)


def orthonormal(partial_value):
    part_a, part_b = partial_value
    rows_a, rows_b = (
        lax.psum(part_a.astype(jnp.bfloat16), "dp").astype(jnp.float32),
        lax.psum(part_b.astype(jnp.bfloat16), "dp").astype(jnp.float32),
    )
    gram_a, gram_b = (
        lax.psum(gram_of(rows_a).astype(jnp.bfloat16), "tensor").astype(jnp.float32),
        lax.psum(gram_of(rows_b).astype(jnp.bfloat16), "tensor").astype(jnp.float32),
    )
    basis_a = solve_rows(gram_a, rows_a)
    basis_b = solve_rows(gram_b, rows_b)
    return (basis_a, basis_b)


def body(norm_in, query_grad, attn_out, handed, sketch_q, sketch_o):
    upstream = from_behind(handed, "section", -1)
    lefts = (norm_in[0], attn_out[0])
    rights = (query_grad[0], upstream[0])
    basis = orthonormal(partials(tokens_of((sketch_q[0], sketch_o[0]), rights), lefts))
    for iteration in range(POWER):
        other = orthonormal(partials(tokens_of(basis, lefts), rights))
        basis = orthonormal(partials(tokens_of(other, rights), lefts))
    final = partials(tokens_of(basis, lefts), rights)
    raw_a, raw_b = (
        lax.psum(final[0].astype(jnp.bfloat16), "dp").astype(jnp.float32),
        lax.psum(final[1].astype(jnp.bfloat16), "dp").astype(jnp.float32),
    )
    energy_a, energy_b = lax.psum((jnp.sum(raw_a * raw_a), jnp.sum(raw_b * raw_b)), "tensor")
    adapter_aq = raw_a / jnp.sqrt(energy_a / (RANK * HQ) + 1e-06)
    adapter_ao = raw_b / jnp.sqrt(energy_b / (RANK * D) + 1e-06)
    adapter_bq = basis[0] * 16.0
    adapter_bo = basis[1] * 16.0
    return (adapter_bq[None], adapter_aq[None], adapter_bo[None], adapter_ao[None])


def solution(mesh):
    return jax.shard_map(
        body,
        mesh=mesh,
        in_specs=(
            P("section", "dp", "tensor"),
            P("section", "dp", "tensor"),
            P("section", "dp", "tensor"),
            P("section", "dp", "tensor"),
            P("section", None, "tensor"),
            P("section", None, "tensor"),
        ),
        out_specs=(
            P("section", None, "tensor"),
            P("section", None, "tensor"),
            P("section", None, "tensor"),
            P("section", None, "tensor"),
        ),
        check_vma=False,
    )
```

profile of v0, /device:TPU:1, one launch (start us, length us, event | category | flops | bytes accessed | tf_op | source)
XLA Modules:
  0.0 1889.8 jit_solution(17088234802325009747)
XLA Ops:
  7.2 13.8 collective-permute-start
  21.1 1.2 convolution_convert_fusion.43
  22.3 9.7 collective-permute-done
  32.3 13.6 all-reduce.17
  47.7 259.3 %all-reduce.35.cloned.1.call-done = (bf16[64,2048]{1,0:T(8,128)(2,1)}, bf16[64,1024]{1,0:T(8,128)(2,1)}) async-done(((bf16[64,2048]{1,0:T(8,128)(2,1)}, bf16[64,1024]{1,0:T(8,128)(2,1)}), (bf16[64,2048]{1,0:T(8,128)(2,1)}, bf16[64,1024]{1,0:T(8,128)(2,1)})) %all-reduce.35.cloned.1.call-update) | async-done | bytes 393232 | tf_op jit(solution)/shard_map/psum | solution.py:54
  307.0 1.2 convolution_convert_fusion.26
  308.5 13.3 all-reduce.16
  322.0 5.8 cholesky.219
  329.2 4.9 custom-call.21
  334.7 5.8 cholesky.164
  341.9 4.9 custom-call.16
  347.8 11.3 all-reduce.15
  361.0 258.1 %all-reduce.33.cloned.1.call-done = (bf16[64,1024]{1,0:T(8,128)(2,1)}, bf16[64,2048]{1,0:T(8,128)(2,1)}) async-done(((bf16[64,1024]{1,0:T(8,128)(2,1)}, bf16[64,2048]{1,0:T(8,128)(2,1)}), (bf16[64,1024]{1,0:T(8,128)(2,1)}, bf16[64,2048]{1,0:T(8,128)(2,1)})) %all-reduce.33.cloned.1.call-update) | async-done | bytes 393232 | tf_op jit(solution)/shard_map/psum | solution.py:54
  619.1 1.2 convolution_convert_fusion.31
  620.5 13.3 all-reduce.14
  634.0 5.8 cholesky.230
  641.2 4.9 custom-call.22
  646.8 5.8 cholesky.175
  654.0 4.9 custom-call.17
  659.9 11.3 all-reduce.13
  671.1 0.9 convolution_convert_fusion.8
  673.0 258.3 %all-reduce.31.cloned.1.call-done = (bf16[64,2048]{1,0:T(8,128)(2,1)}, bf16[64,1024]{1,0:T(8,128)(2,1)}) async-done(((bf16[64,2048]{1,0:T(8,128)(2,1)}, bf16[64,1024]{1,0:T(8,128)(2,1)}), (bf16[64,2048]{1,0:T(8,128)(2,1)}, bf16[64,1024]{1,0:T(8,128)(2,1)})) %all-reduce.31.cloned.1.call-update) | async-done | bytes 393232 | tf_op jit(solution)/shard_map/psum | solution.py:54
  931.3 1.2 convolution_convert_fusion.24
  932.7 13.5 all-reduce.12
  946.3 5.8 cholesky.241
  953.5 4.9 custom-call.23
  959.1 5.8 cholesky.186
  966.3 4.9 custom-call.18
  972.2 11.3 all-reduce.11
  985.4 258.1 %all-reduce.29.cloned.1.call-done = (bf16[64,1024]{1,0:T(8,128)(2,1)}, bf16[64,2048]{1,0:T(8,128)(2,1)}) async-done(((bf16[64,1024]{1,0:T(8,128)(2,1)}, bf16[64,2048]{1,0:T(8,128)(2,1)}), (bf16[64,1024]{1,0:T(8,128)(2,1)}, bf16[64,2048]{1,0:T(8,128)(2,1)})) %all-reduce.29.cloned.1.call-update) | async-done | bytes 393232 | tf_op jit(solution)/shard_map/psum | solution.py:54
  1243.5 1.2 convolution_convert_fusion.29
  1244.9 13.3 all-reduce.10
  1258.3 5.8 cholesky.252
  1265.5 4.9 custom-call.24
  1271.2 5.8 cholesky.197
  1278.4 4.9 custom-call.19
  1284.2 11.3 all-reduce.9
  1297.3 258.3 %all-reduce.27.cloned.1.call-done = (bf16[64,2048]{1,0:T(8,128)(2,1)}, bf16[64,1024]{1,0:T(8,128)(2,1)}) async-done(((bf16[64,2048]{1,0:T(8,128)(2,1)}, bf16[64,1024]{1,0:T(8,128)(2,1)}), (bf16[64,2048]{1,0:T(8,128)(2,1)}, bf16[64,1024]{1,0:T(8,128)(2,1)})) %all-reduce.27.cloned.1.call-update) | async-done | bytes 393232 | tf_op jit(solution)/shard_map/psum | solution.py:54
  1555.6 1.2 convolution_convert_fusion.22
  1557.0 13.5 all-reduce.8
  1570.6 5.8 cholesky.263
  1577.8 4.9 custom-call.25
  1583.4 5.8 cholesky.208
  1590.6 4.9 custom-call.20
  1596.5 11.4 all-reduce.7
  1610.3 257.6 %all-reduce.25.cloned.1.call-done = (bf16[64,1024]{1,0:T(8,128)(2,1)}, bf16[64,2048]{1,0:T(8,128)(2,1)}) async-done(((bf16[64,1024]{1,0:T(8,128)(2,1)}, bf16[64,2048]{1,0:T(8,128)(2,1)}), (bf16[64,1024]{1,0:T(8,128)(2,1)}, bf16[64,2048]{1,0:T(8,128)(2,1)})) %all-reduce.25.cloned.1.call-update) | async-done | bytes 393232 | tf_op jit(solution)/shard_map/psum | solution.py:76
  1867.9 1.7 fusion
  1870.9 9.1 all-reduce
  (135 shorter events, 37.1 us)
Async XLA Ops:
  7.2 38.7 %copy-start = (bf16[1,128,2048]{2,1,0:T(8,128)(2,1)S(1)}, bf16[1,128,2048]{2,1,0:T(8,128)(2,1)}, u32[]{:S(2)}) copy-start(bf16[1,128,2048]{2,1,0:T(8,128)(2,1)} %param.11) | copy-start | bytes 1572868
  7.2 24.8 %copy-start.15 = (bf16[1,64,2048]{2,1,0:T(8,128)(2,1)S(1)}, bf16[1,64,2048]{2,1,0:T(8,128)(2,1)}, u32[]{:S(2)}) copy-start(bf16[1,64,2048]{2,1,0:T(8,128)(2,1)} %param.16) | copy-start | bytes 786436
  7.2 299.9 %all-reduce.35.cloned.1.call-start = ((), (), s32[]{:S(2)}) async-start(), calls=%async_computation.5 | async-start | bytes 786432 | tf_op jit(solution)/shard_map/psum | solution.py:54
  7.2 24.7 %collective-permute-start = (bf16[1,128,2048]{2,1,0:T(8,128)(2,1)}, bf16[1,128,2048]{2,1,0:T(8,128)(2,1)S(1)}, u32[]{:S(2)}, u32[]{:S(2)}) collective-permute-start(bf16[1,128,2048]{2,1,0:T(8,128)(2,1)} %param.14), channel_id=1, source_target_pairs={{0,448},{64,0},{128,64},{192,128},{256,192},{320,256},{384,320},{4... | collective-permute-start | bytes 1572872 | tf_op jit(solution)/shard_map/ppermute | solution.py:18
  45.9 1.0 copy-start.1
  47.7 571.4 %all-reduce.33.cloned.1.call-start = ((), (), s32[]{:S(2)}) async-start(), calls=%async_computation.4 | async-start | bytes 786432 | tf_op jit(solution)/shard_map/psum | solution.py:54
  307.0 1.2 copy-start.3
  322.0 12.1 copy-start.10
  347.5 11.7 copy-start.2
  360.9 570.4 %all-reduce.31.cloned.1.call-start = ((), (), s32[]{:S(2)}) async-start(), calls=%async_computation.3 | async-start | bytes 786432 | tf_op jit(solution)/shard_map/psum | solution.py:54
  619.1 1.2 copy-start.6
  646.7 12.2 copy-start.8
  672.9 570.5 %all-reduce.29.cloned.1.call-start = ((), (), s32[]{:S(2)}) async-start(), calls=%async_computation.2 | async-start | bytes 786432 | tf_op jit(solution)/shard_map/psum | solution.py:54
  931.3 1.2 copy-start.4
  932.7 25.7 %copy-start.11 = (bf16[64,1024]{1,0:T(8,128)(2,1)S(1)}, bf16[64,1024]{1,0:T(8,128)(2,1)}, u32[]{:S(2)}) copy-start(bf16[64,1024]{1,0:T(8,128)(2,1)} %get-tuple-element.16) | copy-start | bytes 393220
  985.3 570.3 %all-reduce.27.cloned.1.call-start = ((), (), s32[]{:S(2)}) async-start(), calls=%async_computation.1 | async-start | bytes 786432 | tf_op jit(solution)/shard_map/psum | solution.py:54
  1243.5 1.2 copy-start.7
  1271.1 12.2 copy-start.9
  1297.3 570.6 %all-reduce.25.cloned.1.call-start = ((), (), s32[]{:S(2)}) async-start(), calls=%async_computation | async-start | bytes 786432 | tf_op jit(solution)/shard_map/psum | solution.py:76
  1555.6 1.2 copy-start.5
  1557.0 25.7 %copy-start.12 = (bf16[64,1024]{1,0:T(8,128)(2,1)S(1)}, bf16[64,1024]{1,0:T(8,128)(2,1)}, u32[]{:S(2)}) copy-start(bf16[64,1024]{1,0:T(8,128)(2,1)} %get-tuple-element.12) | copy-start | bytes 393220
  1867.9 1.7 copy-start.14
  1869.6 11.1 copy-start.13
Sparse Core Ops, SparseCore 0:
  47.8 259.1 all-reduce.34
  361.1 258.0 all-reduce.32
  673.0 258.2 all-reduce.30
  985.4 257.9 all-reduce.28
  1297.4 258.1 all-reduce.26
  1609.7 258.1 all-reduce.24
where the time goes:
time: 1890 us
  waiting for transfers between devices  1560 us (83%)
  blocking collectives  146 us (8%)
  other arithmetic  126 us (7%)
  matrix products  26.9 us (1%)
    psum x5, waiting for transfers between devices, orthonormal(): lax.psum(part_a.astype(jnp.bfloat16), 'dp').astype(jnp.float32)  1290 us
    psum x1, waiting for transfers between devices, body(): lax.psum(final[0].astype(jnp.bfloat16), 'dp').astype(jnp.float32)  258 us
    psum x6, blocking collectives, tokens_of(): lax.psum(first_part.astype(jnp.bfloat16), 'tensor').astype(jnp.float32)  70.2 us
    psum x5, blocking collectives, orthonormal(): lax.psum(gram_of(rows_a).astype(jnp.bfloat16), 'tensor').astype(jnp.float32)  66.9 us
    another operation x30, other arithmetic, solve_rows(): low_factor = jnp.linalg.cholesky(gram_rows)  65.2 us
    another operation x20, other arithmetic, solve_rows(): lax.linalg.triangular_solve(low_factor, row_block, left_side=True, lower=...  55.5 us
  transfers between devices with their start and end apart: 7, of which 7 were waited for; matrix products, arithmetic and copies ran while one was open for 0% of the time, Pallas kernels for 0%

commit v1 on v0

v1 whole, which is shorter than its diff:
```python
import functools

import jax
import jax.numpy as jnp
from jax import lax
from jax.experimental import pallas as pl
from jax.experimental.pallas import tpu as pltpu
from jax.sharding import PartitionSpec as P

RANK = 64
POWER = 2
STAGES = 2 * POWER + 2
NY = 4
GROUP = 8
MESH = pl.DeviceIdType.MESH
f32 = jnp.float32
bf16 = jnp.bfloat16
precise = lax.Precision.HIGHEST


def dot_rows(a, b):
    return lax.dot_general(a, b, (((1,), (1,)), ((), ())), preferred_element_type=f32)


def eliminate(blocks):
    sub = lax.broadcasted_iota(jnp.int32, (8, 128), 0)

    def one_block(b, rows):
        rows = list(rows)
        live = [jnp.where(p + b < 8, 1.0, 0.0).astype(f32) for p in range(1, 8)]
        for i in range(8):
            row = jnp.broadcast_to(rows[0][i : i + 1, :], (8, 128))
            root = lax.rsqrt(jnp.broadcast_to(row[:, i : i + 1], (8, 128)))
            unit = row * root
            scaled = unit * root
            head = rows[0]
            lower = head - jnp.broadcast_to(head[:, i : i + 1], (8, 128)) * scaled
            for p in range(1, 8):
                column = jnp.broadcast_to(rows[p][:, i : i + 1], (8, 128))
                rows[p] = rows[p] - (column * live[p - 1]) * scaled
            rows[0] = jnp.where(sub == i, unit, jnp.where(sub > i, lower, head))
        rows = [pltpu.roll(r, 120, 1) for r in rows]
        return tuple(rows[1:] + rows[:1])

    return lax.fori_loop(0, 8, one_block, tuple(blocks))


def kernel(
    norm_ref, query_ref, attn_ref, handed_ref, sk_q_ref, sk_o_ref,
    b_q_ref, a_q_ref, b_o_ref, a_o_ref,
    up, y_buf, e_buf, inv_buf, scale_buf, send_w, send_n, recv_w, recv_n, z_w, z_n, all_w, all_n,
    up_sems, y_send, y_recv, rs_send, rs_recv, z_send, z_recv, ag_send, ag_recv, e_send, e_recv,
):
    section = lax.axis_index("section")
    dp = lax.axis_index("dp")
    y = lax.axis_index("tensor")
    sections = lax.axis_size("section")
    x, z, core = dp // 4, (dp // 2) % 2, dp % 2
    me = x * 2 + core
    behind, ahead = (section + sections - 1) % sections, (section + 1) % sections

    def y_peer(r):
        return {"tensor": (y + r) % NY}

    def group_peer(r):
        other = (me + r) % GROUP
        return {"dp": ((other // 2) * 2 + z) * 2 + other % 2}

    z_peer = {"dp": (x * 2 + (1 - z)) * 2 + core}

    barrier = pltpu.get_barrier_semaphore()
    peers = [{"section": behind}, {"section": ahead}, z_peer]
    peers += [y_peer(r) for r in range(1, NY)] + [group_peer(r) for r in range(1, GROUP)]
    for peer in peers:
        pl.semaphore_signal(barrier, inc=1, device_id=peer, device_id_type=MESH)
    pl.semaphore_wait(barrier, len(peers))

    def remote(src, dst, sent, received, peer):
        copy = pltpu.make_async_remote_copy(
            src_ref=src, dst_ref=dst, send_sem=sent, recv_sem=received, device_id=peer, device_id_type=MESH
        )
        copy.start()
        return copy

    pending = []
    shift = remote(handed_ref, up, up_sems.at[0], up_sems.at[1], {"section": behind})
    pending.append(shift)

    def chain(c, left, right, sketch, b_out, a_out):
        for k in range(STAGES):
            before, here = (right, left) if k % 2 == 0 else (left, right)
            wide = here.shape[2] // GROUP
            big = wide == 256
            slot = c * 3 + k // 2
            mine, theirs, z_b, everyone = (
                (send_w, recv_w, z_w, all_w) if big else (send_n, recv_n, z_n, all_n)
            )
            mine, theirs, z_b, everyone = mine.at[slot], theirs.at[slot], z_b.at[slot], everyone.at[slot]
            idx = c * STAGES + k

            if k == 0:
                part = dot_rows(sketch[0], before[0])
                y_buf[idx, y, :RANK, :] = part.astype(bf16)
                span = RANK
            else:
                both = None
                width = before.shape[2] // GROUP
                for j in range(GROUP):
                    piece = last[j]
                    stacked = jnp.concatenate([before[0, :, j * width : (j + 1) * width], piece, piece], axis=0)
                    term = dot_rows(piece, stacked)
                    both = term if both is None else both + term
                y_buf[idx, y, :RANK, :] = both[:, :128].astype(bf16)
                gram = both[:, 128:]
                high = gram.astype(bf16)
                rest = (gram - high.astype(f32)).astype(bf16)
                lane = lax.broadcasted_iota(jnp.int32, (RANK, 128), 1)
                y_buf[idx, y, RANK:, :] = jnp.where(lane < RANK, high.astype(f32), rest.astype(f32)).astype(bf16)
                span = 2 * RANK
            own = y_buf.at[idx, y, pl.ds(0, span)]
            copies = [
                remote(own, own, y_send.at[idx, r - 1], y_recv.at[idx, r - 1], y_peer(r)) for r in range(1, NY)
            ]
            pending.extend(copies)
            yield
            for copy in copies:
                copy.wait_recv()
            token_sum = y_buf[idx, 0, :RANK, :].astype(f32)
            for j in range(1, NY):
                token_sum = token_sum + y_buf[idx, j, :RANK, :].astype(f32)
            blocks = None
            if k > 0:
                packed = y_buf[idx, 0, RANK:, :].astype(f32)
                for j in range(1, NY):
                    packed = packed + y_buf[idx, j, RANK:, :].astype(f32)
                gram = packed + pltpu.roll(packed, RANK, 1)
                line = lax.broadcasted_iota(jnp.int32, (RANK, 128), 0)
                lane = lax.broadcasted_iota(jnp.int32, (RANK, 128), 1)
                diagonal = jnp.where(line == lane, gram, 0.0)
                by_row = lax.rsqrt(jnp.sum(diagonal, axis=1, keepdims=True))
                column_diagonal = jnp.where((line == lane) | (line + RANK == lane), gram, 0.0)
                by_lane = lax.rsqrt(jnp.sum(column_diagonal, axis=0, keepdims=True))
                token_sum = token_sum * by_row
                scaled = gram * by_row * by_lane
                augmented = jnp.where(lane < RANK, scaled, jnp.where(line + RANK == lane, 1.0, 0.0))
                inv_buf[c] = augmented
                scale_buf[c] = jnp.broadcast_to(by_lane, (8, 128))
            rows = token_sum.astype(bf16)
            for j in range(GROUP):
                piece = jnp.dot(rows, here[0, :, j * wide : (j + 1) * wide], preferred_element_type=f32)
                mine[j] = piece.astype(bf16)
            copies = []
            for r in range(1, GROUP):
                other = (me + r) % GROUP
                copies.append(
                    remote(
                        mine.at[other], theirs.at[me], rs_send.at[idx, r - 1], rs_recv.at[idx, r - 1], group_peer(r)
                    )
                )
            pending.extend(copies)
            theirs[me] = mine[me]
            yield
            for copy in copies:
                copy.wait_recv()
            total = theirs[0].astype(f32)
            for j in range(1, GROUP):
                total = total + theirs[j].astype(f32)
            z_b[0] = total.astype(bf16)
            copy = remote(z_b.at[0], z_b.at[1], z_send.at[idx], z_recv.at[idx], z_peer)
            pending.append(copy)
            if k > 0:
                reduced = eliminate([inv_buf[c, 8 * p : 8 * p + 8, :] for p in range(8)])
                for p in range(8):
                    inv_buf[c, 8 * p : 8 * p + 8, :] = reduced[p]
                if k == STAGES - 1:
                    inverse = inv_buf[c][:, :RANK] * scale_buf[c][:1, :RANK]
                    width = before.shape[2] // GROUP
                    for j in range(GROUP):
                        basis = jnp.dot(
                            inverse, last[j].astype(f32), precision=precise, preferred_element_type=f32
                        )
                        b_out[0, :, j * width : (j + 1) * width] = (basis.astype(bf16).astype(f32) * 16.0).astype(bf16)
            yield
            copy.wait_recv()
            total = z_b[0].astype(f32) + z_b[1].astype(f32)
            if k > 0:
                total = jnp.dot(inv_buf[c][:, :RANK], total, precision=precise, preferred_element_type=f32)
            everyone[me] = total.astype(bf16)
            own = everyone.at[me]
            copies = [
                remote(own, own, ag_send.at[idx, r - 1], ag_recv.at[idx, r - 1], group_peer(r))
                for r in range(1, GROUP)
            ]
            pending.extend(copies)
            yield
            for copy in copies:
                copy.wait_recv()
            last = everyone
        energy = None
        for j in range(GROUP):
            value = last[j].astype(f32)
            value = value * value
            for i in range(8):
                for lanes in range(0, value.shape[1], 128):
                    term = value[8 * i : 8 * i + 8, lanes : lanes + 128]
                    energy = term if energy is None else energy + term
        e_buf[c, y] = energy
        own = e_buf.at[c, y]
        copies = [remote(own, own, e_send.at[c, r - 1], e_recv.at[c, r - 1], y_peer(r)) for r in range(1, NY)]
        pending.extend(copies)
        yield
        for copy in copies:
            copy.wait_recv()
        energy = e_buf[c, 0] + e_buf[c, 1] + e_buf[c, 2] + e_buf[c, 3]
        energy = jnp.sum(jnp.sum(energy, axis=1, keepdims=True), axis=0, keepdims=True)
        columns = GROUP * wide * NY
        factor = 1.0 / jnp.sqrt(energy / (RANK * columns) + 1e-06)
        for j in range(GROUP):
            a_out[0, :, j * wide : (j + 1) * wide] = last[j].astype(f32) * factor
        yield

    first = chain(0, norm_ref, query_ref, sk_q_ref, b_q_ref, a_q_ref)
    second = chain(1, attn_ref, up, sk_o_ref, b_o_ref, a_o_ref)
    for _ in range(3):
        next(first)
    shift.wait_recv()
    next(second)
    order = []
    for _ in range(STAGES - 1):
        order += [1, 0, 1, 0, 0, 1, 0, 1]
    order += [1, 0, 1, 0, 0, 1, 1, 1]
    chains = (first, second)
    for which in order:
        next(chains[which])
    for copy in pending:
        copy.wait_send()


def body(*operands):
    norm_in, query_grad, attn_out, handed, sketch_q, sketch_o = operands
    dim, features = norm_in.shape[2], query_grad.shape[2]
    tokens = norm_in.shape[1]
    vmem = pl.BlockSpec(memory_space=pltpu.VMEM)
    wide, narrow = dim // GROUP, features // GROUP
    dma = pltpu.SemaphoreType.DMA
    n = 2 * STAGES
    out_shape = (
        jax.ShapeDtypeStruct((1, RANK, dim), bf16),
        jax.ShapeDtypeStruct((1, RANK, features), f32),
        jax.ShapeDtypeStruct((1, RANK, features), bf16),
        jax.ShapeDtypeStruct((1, RANK, dim), f32),
    )
    scratch = [
        pltpu.VMEM((1, tokens, dim), bf16),
        pltpu.VMEM((n, NY, 2 * RANK, 128), bf16),
        pltpu.VMEM((2, NY, 8, 128), f32),
        pltpu.VMEM((2, RANK, 128), f32),
        pltpu.VMEM((2, 8, 128), f32),
        pltpu.VMEM((STAGES, GROUP, RANK, wide), bf16),
        pltpu.VMEM((STAGES, GROUP, RANK, narrow), bf16),
        pltpu.VMEM((STAGES, GROUP, RANK, wide), bf16),
        pltpu.VMEM((STAGES, GROUP, RANK, narrow), bf16),
        pltpu.VMEM((STAGES, 2, RANK, wide), bf16),
        pltpu.VMEM((STAGES, 2, RANK, narrow), bf16),
        pltpu.VMEM((STAGES, GROUP, RANK, wide), bf16),
        pltpu.VMEM((STAGES, GROUP, RANK, narrow), bf16),
        dma((2,)),
        dma((n, NY - 1)),
        dma((n, NY - 1)),
        dma((n, GROUP - 1)),
        dma((n, GROUP - 1)),
        dma((n,)),
        dma((n,)),
        dma((n, GROUP - 1)),
        dma((n, GROUP - 1)),
        dma((2, NY - 1)),
        dma((2, NY - 1)),
    ]
    return pl.pallas_call(
        kernel,
        out_shape=out_shape,
        in_specs=[vmem] * 6,
        out_specs=(vmem,) * 4,
        scratch_shapes=scratch,
        compiler_params=pltpu.CompilerParams(
            collective_id=0, has_side_effects=True, vmem_limit_bytes=40 * 1024 * 1024
        ),
        name="adapters",
    )(*operands)


def solution(mesh):
    row = P("section", "dp", "tensor")
    thin = P("section", None, "tensor")
    return jax.shard_map(
        body,
        mesh=mesh,
        in_specs=(row, row, row, row, thin, thin),
        out_specs=(thin, thin, thin, thin),
        check_vma=False,
    )
```

time: 1890 us -> 249 us (0.13)
  waiting for transfers between devices: 1560 us -> 0 us
  Pallas kernels: 0 us -> 239 us
  blocking collectives: 146 us -> 0 us
  other arithmetic: 126 us -> 0 us
  matrix products: 26.9 us -> 0 us
    psum x6 -> x0, waiting for transfers between devices: 1550 us -> none  [the longest x5 1290 us: orthonormal(): lax.psum(part_a.astype(jnp.bfloat16), 'dp').astype(jnp.float32)]
    pallas_call x0 -> x1, Pallas kernels: none -> 239 us  [body(): pl.pallas_call(kernel, out_shape=out_shape, in_specs=[vmem] * 6, out_spec...]
    psum x12 -> x0, blocking collectives: 146 us -> none  [the longest x6 70.2 us: tokens_of(): lax.psum(first_part.astype(jnp.bfloat16), 'tensor').astype(jnp.float32)]
    another operation x50 -> x0, other arithmetic: 121 us -> none  [the longest x30 65.2 us: solve_rows(): low_factor = jnp.linalg.cholesky(gram_rows)]
    dot_general x34 -> x0, matrix products: 21.6 us -> none  [the longest x10 6.97 us: gram_of(): jnp.dot(row_block, row_block.T, precision=precise, preferred_element_type...]
  transfers between devices with their start and end apart: 7 -> 0, of which waited for: 7 -> 0; matrix products, arithmetic and copies ran while one was open for 0% -> 0% of each run, Pallas kernels for 0% -> 0%
where the time goes in v1:
time: 249 us; the launch traced here: 248 us
  Pallas kernels  239 us (96%)
  local copies, waits for them, and re-layouts  8.68 us (3%)
    pallas_call x1, Pallas kernels, body(): pl.pallas_call(kernel, out_shape=out_shape, in_specs=[vmem] * 6, out_spec...  239 us
    unnamed x16, local copies, waits for them, and re-layouts  8.68 us

profile of v1, /device:TPU:1, one launch (start us, length us, event | category | flops | bytes accessed | tf_op | source)
XLA Modules:
  0.0 248.3 jit_solution(4942226521811584758)
XLA Ops:
  0.6 0.0 copy-start
  0.6 1.0 copy-done
  1.7 0.0 copy-start.1
  1.7 1.0 copy-done.1
  2.7 0.0 copy-start.2
  2.7 0.9 copy-done.2
  3.7 0.0 copy-start.3
  3.7 0.9 copy-done.3
  4.6 0.0 copy-start.4
  4.6 0.9 copy-done.4
  5.6 0.0 copy-start.5
  5.6 0.9 copy-done.5
  6.5 239.0 %adapters.1 = (bf16[1,64,2048]{2,1,0:T(8,128)(2,1)S(1)}, f32[1,64,1024]{2,1,0:T(8,128)S(1)}, bf16[1,64,1024]{2,1,0:T(8,128)(2,1)S(1)}, f32[1,64,2048]{2,1,0:T(8,128)S(1)}) custom-call(bf16[1,128,2048]{2,1,0:T(8,128)(2,1)S(1)} %copy-done, bf16[1,128,1024]{2,1,0:T(8,128)(2,1)S(1)} %copy-done.2, bf16[1,128,1024]{2,1,0:T(8,128)(2,1)S(1)} %copy-done.3, ...), custom_call_target="tpu_custom_call" | custom-call | tf_op jit(solution)/shard_map/adapters/pallas_call | solution.py:279
  245.4 0.7 copy.14
  246.2 0.7 copy.15
  246.9 0.7 copy.16
  247.5 0.8 copy.17
Async XLA Ops:
  0.6 1.0 copy-start
  1.7 1.0 copy-start.1
  2.7 0.9 copy-start.2
  3.7 0.9 copy-start.3
  4.6 0.9 copy-start.4
  5.6 0.9 copy-start.5

commit v2 on v1

--- a/solution.py
+++ b/solution.py
@@ -25,20 +25,33 @@
 def eliminate(blocks):
     sub = lax.broadcasted_iota(jnp.int32, (8, 128), 0)
 
+    def across(value, i):
+        return jnp.broadcast_to(value[:, i : i + 1], (8, 128))
+
+    def down(value, i):
+        return jnp.broadcast_to(value[i : i + 1, :], (8, 128))
+
     def one_block(b, rows):
         rows = list(rows)
-        live = [jnp.where(p + b < 8, 1.0, 0.0).astype(f32) for p in range(1, 8)]
+        work = done = rows[0]
+        columns = [across(work, i) for i in range(8)]
         for i in range(8):
-            row = jnp.broadcast_to(rows[0][i : i + 1, :], (8, 128))
-            root = lax.rsqrt(jnp.broadcast_to(row[:, i : i + 1], (8, 128)))
-            unit = row * root
-            scaled = unit * root
-            head = rows[0]
-            lower = head - jnp.broadcast_to(head[:, i : i + 1], (8, 128)) * scaled
-            for p in range(1, 8):
-                column = jnp.broadcast_to(rows[p][:, i : i + 1], (8, 128))
-                rows[p] = rows[p] - (column * live[p - 1]) * scaled
-            rows[0] = jnp.where(sub == i, unit, jnp.where(sub > i, lower, head))
+            pivot = down(columns[i], i)
+            root = lax.rsqrt(pivot)
+            row = down(work, i)
+            done = jnp.where(sub == i, row * root, done)
+            step = jnp.where(sub == i, pivot - 1.0, columns[i]) * (root * root)
+            for j in range(i + 1, 8):
+                columns[j] = columns[j] - down(columns[j], i) * step
+            work = work - row * step
+        solved = [down(work, i) for i in range(8)]
+        for p in range(1, 8):
+            change = across(rows[p], 0) * solved[0]
+            for i in range(1, 8):
+                change = change + across(rows[p], i) * solved[i]
+            live = jnp.where(p + b < 8, 1.0, 0.0).astype(f32)
+            rows[p] = rows[p] - change * live
+        rows[0] = done
         rows = [pltpu.roll(r, 120, 1) for r in rows]
         return tuple(rows[1:] + rows[:1])
 
@@ -46,10 +59,10 @@
 
 
 def kernel(
-    norm_ref, query_ref, attn_ref, handed_ref, sk_q_ref, sk_o_ref,
+    norm_hbm, query_hbm, attn_hbm, handed_hbm, sk_q_hbm, sk_o_hbm,
     b_q_ref, a_q_ref, b_o_ref, a_o_ref,
-    up, y_buf, e_buf, inv_buf, scale_buf, send_w, send_n, recv_w, recv_n, z_w, z_n, all_w, all_n,
-    up_sems, y_send, y_recv, rs_send, rs_recv, z_send, z_recv, ag_send, ag_recv, e_send, e_recv,
+    norm_ref, query_ref, attn_ref, sk_q_ref, sk_o_ref, up, y_buf, e_buf, inv_buf, scale_buf, send_w, send_n, recv_w, recv_n, z_w, z_n, all_w, all_n,
+    up_sems, y_send, y_recv, rs_send, rs_recv, z_send, z_recv, ag_send, ag_recv, e_send, e_recv, in_sems,
 ):
     section = lax.axis_index("section")
     dp = lax.axis_index("dp")
@@ -68,6 +81,17 @@
 
     z_peer = {"dp": (x * 2 + (1 - z)) * 2 + core}
 
+    loads = [
+        pltpu.make_async_copy(source, target, in_sems.at[i])
+        for i, (source, target) in enumerate(
+            (
+                (query_hbm, query_ref), (sk_q_hbm, sk_q_ref), (norm_hbm, norm_ref),
+                (sk_o_hbm, sk_o_ref), (attn_hbm, attn_ref),
+            )
+        )
+    ]
+    for load in loads:
+        load.start()
     barrier = pltpu.get_barrier_semaphore()
     peers = [{"section": behind}, {"section": ahead}, z_peer]
     peers += [y_peer(r) for r in range(1, NY)] + [group_peer(r) for r in range(1, GROUP)]
@@ -83,8 +107,10 @@
         return copy
 
     pending = []
-    shift = remote(handed_ref, up, up_sems.at[0], up_sems.at[1], {"section": behind})
+    shift = remote(handed_hbm, up, up_sems.at[0], up_sems.at[1], {"section": behind})
     pending.append(shift)
+    for load in loads:
+        load.wait()
 
     def chain(c, left, right, sketch, b_out, a_out):
         for k in range(STAGES):
@@ -251,6 +277,11 @@
         jax.ShapeDtypeStruct((1, RANK, dim), f32),
     )
     scratch = [
+        pltpu.VMEM(norm_in.shape, bf16),
+        pltpu.VMEM(query_grad.shape, bf16),
+        pltpu.VMEM(attn_out.shape, bf16),
+        pltpu.VMEM(sketch_q.shape, bf16),
+        pltpu.VMEM(sketch_o.shape, bf16),
         pltpu.VMEM((1, tokens, dim), bf16),
         pltpu.VMEM((n, NY, 2 * RANK, 128), bf16),
         pltpu.VMEM((2, NY, 8, 128), f32),
@@ -275,15 +306,16 @@
         dma((n, GROUP - 1)),
         dma((2, NY - 1)),
         dma((2, NY - 1)),
+        dma((5,)),
     ]
     return pl.pallas_call(
         kernel,
         out_shape=out_shape,
-        in_specs=[vmem] * 6,
+        in_specs=[pl.BlockSpec(memory_space=pltpu.HBM)] * 6,
         out_specs=(vmem,) * 4,
         scratch_shapes=scratch,
         compiler_params=pltpu.CompilerParams(
-            collective_id=0, has_side_effects=True, vmem_limit_bytes=40 * 1024 * 1024
+            collective_id=0, has_side_effects=True, vmem_limit_bytes=65800000
         ),
         name="adapters",
     )(*operands)

time: 249 us -> 190 us (0.76)
  Pallas kernels: 239 us -> 184 us
  local copies, waits for them, and re-layouts: 8.68 us -> 4.19 us
    pallas_call x1, Pallas kernels: 239 us -> 184 us  [body(): pl.pallas_call(kernel, out_shape=out_shape, in_specs=[pl.BlockSpec(memory...]
    unnamed x16 -> x10, local copies, waits for them, and re-layouts: 8.68 us -> 4.19 us
where the time goes in v2:
time: 190 us; the launch traced here: 189 us
  Pallas kernels  184 us (97%)
  local copies, waits for them, and re-layouts  4.19 us (2%)
    pallas_call x1, Pallas kernels, body(): pl.pallas_call(kernel, out_shape=out_shape, in_specs=[pl.BlockSpec(memory...  184 us
    unnamed x10, local copies, waits for them, and re-layouts  4.19 us

profile of v2, /device:TPU:1, one launch (start us, length us, event | category | flops | bytes accessed | tf_op | source)
XLA Modules:
  0.0 189.2 jit_solution(7111539589653979655)
XLA Ops:
  0.6 184.3 %adapters.1 = (bf16[1,64,2048]{2,1,0:T(8,128)(2,1)}, f32[1,64,1024]{2,1,0:T(8,128)}, bf16[1,64,1024]{2,1,0:T(8,128)(2,1)}, f32[1,64,2048]{2,1,0:T(8,128)}) custom-call(bf16[1,128,2048]{2,1,0:T(8,128)(2,1)} %norm_hbm.1, bf16[1,128,1024]{2,1,0:T(8,128)(2,1)} %query_hbm.1, bf16[1,128,1024]{2,1,0:T(8,128)(2,1)} %attn_hbm.1, bf16[1,128,2048]{2,1,0:T(8,128)(2,1)} %handed_hbm.1, ...), custom_call_target="tpu_custom_call" | custom-call | tf_op jit(solution)/shard_map/adapters/pallas_call | solution.py:311
  185.0 0.0 copy-start.1
  185.0 0.0 copy-start
  185.0 1.7 copy.14
  186.7 0.0 copy-done.1
  186.7 0.0 copy-start.2
  186.7 0.7 copy.15
  187.4 0.3 copy-done.2
  187.7 0.7 copy.16
  188.4 0.0 copy-done
  188.4 0.8 copy.17
Async XLA Ops:
  185.0 1.8 copy-start.1
  185.0 3.4 %copy-start = (f32[1,64,2048]{2,1,0:T(8,128)S(1)}, f32[1,64,2048]{2,1,0:T(8,128)}, u32[]{:S(2)}) copy-start(f32[1,64,2048]{2,1,0:T(8,128)} %get-tuple-element.11) | copy-start | bytes 1572868
  186.7 1.0 copy-start.2

commit v3 on v2

v3 whole, which is shorter than its diff:
```python
import functools

import jax
import jax.numpy as jnp
from jax import lax
from jax.experimental import pallas as pl
from jax.experimental.pallas import tpu as pltpu
from jax.sharding import PartitionSpec as P

RANK = 64
POWER = 2
STAGES = 2 * POWER + 2
NY = 4
GROUP = 8
MESH = pl.DeviceIdType.MESH
ORDER = [
    0, 0, 0, 2, 1, 1, 1, 0, 1, 0, 1, 0, 1, 0, 0, 1, 1, 0, 1, 0, 0, 1, 0, 1,
    0, 1, 1, 0, 1, 0, 1, 0, 1, 0, 0, 1, 1, 0, 1, 0, 0, 1, 0, 1, 0, 1, 1, 0,
    1, 0, 1, 0, 1, 0, 1, 0, 1, 0, 0, 1, 0, 1, 1, 1,
]
f32 = jnp.float32
bf16 = jnp.bfloat16
precise = lax.Precision.HIGHEST


def dot_rows(a, b):
    return lax.dot_general(a, b, (((1,), (1,)), ((), ())), preferred_element_type=f32)


def eliminate(blocks):
    sub = lax.broadcasted_iota(jnp.int32, (8, 128), 0)

    def across(value, i):
        return jnp.broadcast_to(value[:, i : i + 1], (8, 128))

    def down(value, i):
        return jnp.broadcast_to(value[i : i + 1, :], (8, 128))

    def one_block(b, rows):
        rows = list(rows)
        work = done = rows[0]
        columns = [across(work, i) for i in range(8)]
        for i in range(8):
            pivot = down(columns[i], i)
            root = lax.rsqrt(pivot)
            row = down(work, i)
            done = jnp.where(sub == i, row * root, done)
            step = jnp.where(sub == i, pivot - 1.0, columns[i]) * (root * root)
            for j in range(i + 1, 8):
                columns[j] = columns[j] - down(columns[j], i) * step
            work = work - row * step
        solved = [down(work, i) for i in range(8)]
        for p in range(1, 8):
            change = across(rows[p], 0) * solved[0]
            for i in range(1, 8):
                change = change + across(rows[p], i) * solved[i]
            live = jnp.where(p + b < 8, 1.0, 0.0).astype(f32)
            rows[p] = rows[p] - change * live
        rows[0] = done
        rows = [pltpu.roll(r, 120, 1) for r in rows]
        return tuple(rows[1:] + rows[:1])

    return lax.fori_loop(0, 8, one_block, tuple(blocks))


def kernel(
    norm_hbm, query_hbm, attn_hbm, handed_hbm, sk_q_hbm, sk_o_hbm,
    b_q_ref, a_q_ref, b_o_ref, a_o_ref,
    norm_ref, query_ref, attn_ref, sk_q_ref, sk_o_ref, up, y_buf, g_buf, e_buf, h_buf, inv_buf, send_w, send_n, recv_w, recv_n, z_w, z_n, all_w, all_n,
    up_sems, y_send, y_recv, g_send, g_recv, rs_send, rs_recv, z_send, z_recv, ag_send, ag_recv, e_send, e_recv, h_send, h_recv, in_sems,
):
    section = lax.axis_index("section")
    dp = lax.axis_index("dp")
    y = lax.axis_index("tensor")
    sections = lax.axis_size("section")
    x, z, core = dp // 4, (dp // 2) % 2, dp % 2
    me = x * 2 + core
    behind, ahead = (section + sections - 1) % sections, (section + 1) % sections

    def y_peer(r):
        return {"tensor": (y + r) % NY}

    def group_peer(r):
        other = (me + r) % GROUP
        return {"dp": ((other // 2) * 2 + z) * 2 + other % 2}

    z_peer = {"dp": (x * 2 + (1 - z)) * 2 + core}

    loads = [
        pltpu.make_async_copy(source, target, in_sems.at[i])
        for i, (source, target) in enumerate(
            (
                (query_hbm, query_ref), (sk_q_hbm, sk_q_ref), (norm_hbm, norm_ref),
                (sk_o_hbm, sk_o_ref), (attn_hbm, attn_ref),
            )
        )
    ]
    for load in loads:
        load.start()
    barrier = pltpu.get_barrier_semaphore()
    peers = [{"section": behind}, {"section": ahead}, z_peer]
    peers += [y_peer(r) for r in range(1, NY)] + [group_peer(r) for r in range(1, GROUP)]
    for peer in peers:
        pl.semaphore_signal(barrier, inc=1, device_id=peer, device_id_type=MESH)

    def remote(src, dst, sent, received, peer):
        copy = pltpu.make_async_remote_copy(
            src_ref=src, dst_ref=dst, send_sem=sent, recv_sem=received, device_id=peer, device_id_type=MESH
        )
        copy.start()
        return copy

    pending = []

    def chain(c, left, right, sketch, b_out, a_out, ready):
        for k in range(STAGES):
            before, here = (right, left) if k % 2 == 0 else (left, right)
            wide = here.shape[2] // GROUP
            width = before.shape[2] // GROUP
            slot = c * 3 + k // 2
            buffers = (send_w, recv_w, z_w, all_w) if wide == 256 else (send_n, recv_n, z_n, all_n)
            mine, theirs, z_b, everyone = (buffer.at[slot] for buffer in buffers)
            idx = c * STAGES + k

            if k == 0:
                part = dot_rows(sketch[0], before[0])
            else:
                part = None
                for r in range(GROUP):
                    source = (me + GROUP - r) % GROUP
                    if r > 0:
                        gathers[r - 1].wait_recv()
                    columns = pl.ds(pl.multiple_of(source * width, 128), width)
                    term = dot_rows(last[source], before[0, :, columns])
                    part = term if part is None else part + term
            y_buf[idx, y] = part.astype(bf16)
            ready()
            own = y_buf.at[idx, y]
            factors = [remote(own, own, y_send.at[idx, r - 1], y_recv.at[idx, r - 1], y_peer(r)) for r in range(1, NY)]
            pending.extend(factors)
            if k > 0:
                gram = None
                for j in range(GROUP):
                    piece = last[j]
                    term = dot_rows(piece, jnp.concatenate([piece, piece], axis=0))
                    gram = term if gram is None else gram + term
                high = gram.astype(bf16).astype(f32)
                lane = lax.broadcasted_iota(jnp.int32, (RANK, 128), 1)
                g_buf[idx, y] = jnp.where(lane < RANK, high, gram - high).astype(bf16)
                own = g_buf.at[idx, y]
                grams = [
                    remote(own, own, g_send.at[idx, r - 1], g_recv.at[idx, r - 1], y_peer(r)) for r in range(1, NY)
                ]
                pending.extend(grams)
            yield

            for copy in factors:
                copy.wait_recv()
            token_sum = y_buf[idx, 0].astype(f32)
            for j in range(1, NY):
                token_sum = token_sum + y_buf[idx, j].astype(f32)
            rows = token_sum.astype(bf16)
            scatters = []
            for r in range(1, GROUP + 1):
                other = (me + r) % GROUP
                columns = pl.ds(pl.multiple_of(other * wide, 128), wide)
                piece = jnp.dot(rows, here[0, :, columns], preferred_element_type=f32).astype(bf16)
                if r == GROUP:
                    theirs[me] = piece
                else:
                    mine[other] = piece
                    scatters.append(
                        remote(
                            mine.at[other], theirs.at[me], rs_send.at[idx, r - 1], rs_recv.at[idx, r - 1],
                            group_peer(r),
                        )
                    )
            pending.extend(scatters)
            yield

            for copy in scatters:
                copy.wait_recv()
            total = theirs[0].astype(f32)
            for j in range(1, GROUP):
                total = total + theirs[j].astype(f32)
            z_b[0] = total.astype(bf16)
            exchange = remote(z_b.at[0], z_b.at[1], z_send.at[idx], z_recv.at[idx], z_peer)
            pending.append(exchange)
            yield

            if k > 0:
                for copy in grams:
                    copy.wait_recv()
                packed = g_buf[idx, 0].astype(f32)
                for j in range(1, NY):
                    packed = packed + g_buf[idx, j].astype(f32)
                gram = packed + pltpu.roll(packed, RANK, 1)
                line = lax.broadcasted_iota(jnp.int32, (RANK, 128), 0)
                lane = lax.broadcasted_iota(jnp.int32, (RANK, 128), 1)
                by_row = lax.rsqrt(jnp.sum(jnp.where(line == lane, gram, 0.0), axis=1, keepdims=True))
                diagonal = jnp.where((line == lane) | (line + RANK == lane), gram, 0.0)
                by_lane = lax.rsqrt(jnp.sum(diagonal, axis=0, keepdims=True))
                identity = jnp.where(line + RANK == lane, 1.0, 0.0)
                augmented = jnp.where(lane < RANK, gram * by_row * by_lane, identity)
                reduced = eliminate([augmented[8 * p : 8 * p + 8, :] for p in range(8)])
                for p in range(8):
                    inv_buf[c, 8 * p : 8 * p + 8, :] = reduced[p] * by_lane
                if k == STAGES - 1:
                    inverse = inv_buf[c][:, :RANK]
                    for j in range(GROUP):
                        basis = jnp.dot(
                            inverse, last[j].astype(f32), precision=precise, preferred_element_type=f32
                        )
                        b_out[0, :, j * width : (j + 1) * width] = (basis.astype(bf16).astype(f32) * 16.0).astype(bf16)
            yield

            exchange.wait_recv()
            total = z_b[0].astype(f32) + z_b[1].astype(f32)
            if k > 0:
                total = jnp.dot(inv_buf[c][:, :RANK], total, precision=precise, preferred_element_type=f32)
            total = total.astype(bf16)
            everyone[me] = total
            own = everyone.at[me]
            gathers = [
                remote(own, own, ag_send.at[idx, r - 1], ag_recv.at[idx, r - 1], group_peer(r))
                for r in range(1, GROUP)
            ]
            pending.extend(gathers)
            last = everyone
            if k == STAGES - 1:
                square = total.astype(f32)
                square = square * square
                energy = None
                for i in range(8):
                    for lanes in range(0, wide, 128):
                        term = square[8 * i : 8 * i + 8, lanes : lanes + 128]
                        energy = term if energy is None else energy + term
                e_buf[c, y] = energy
                own = e_buf.at[c, y]
                energies = [
                    remote(own, own, e_send.at[c, r - 1], e_recv.at[c, r - 1], y_peer(r)) for r in range(1, NY)
                ]
                pending.extend(energies)
            yield

        for copy in energies:
            copy.wait_recv()
        h_buf[c, me] = e_buf[c, 0] + e_buf[c, 1] + e_buf[c, 2] + e_buf[c, 3]
        own = h_buf.at[c, me]
        shares = [remote(own, own, h_send.at[c, r - 1], h_recv.at[c, r - 1], group_peer(r)) for r in range(1, GROUP)]
        pending.extend(shares)
        yield
        for copy in gathers + shares:
            copy.wait_recv()
        energy = h_buf[c, 0]
        for j in range(1, GROUP):
            energy = energy + h_buf[c, j]
        energy = jnp.sum(jnp.sum(energy, axis=1, keepdims=True), axis=0, keepdims=True)
        columns = GROUP * wide * NY
        factor = 1.0 / jnp.sqrt(energy / (RANK * columns) + 1e-06)
        for j in range(GROUP):
            a_out[0, :, j * wide : (j + 1) * wide] = last[j].astype(f32) * factor
        yield

    shifts = []

    def begin():
        if not shifts:
            pl.semaphore_wait(barrier, len(peers))
            shifts.append(remote(handed_hbm, up, up_sems.at[0], up_sems.at[1], {"section": behind}))
            pending.extend(shifts)

    loads[0].wait()
    loads[1].wait()
    chains = (
        chain(0, norm_ref, query_ref, sk_q_ref, b_q_ref, a_q_ref, begin),
        chain(1, attn_ref, up, sk_o_ref, b_o_ref, a_o_ref, begin),
    )
    next(chains[0])
    for load in loads[2:]:
        load.wait()
    for which in ORDER:
        if which == 2:
            shifts[0].wait_recv()
        else:
            next(chains[which])
    for copy in pending:
        copy.wait_send()


def body(*operands):
    norm_in, query_grad, attn_out, handed, sketch_q, sketch_o = operands
    dim, features = norm_in.shape[2], query_grad.shape[2]
    tokens = norm_in.shape[1]
    vmem = pl.BlockSpec(memory_space=pltpu.VMEM)
    wide, narrow = dim // GROUP, features // GROUP
    dma = pltpu.SemaphoreType.DMA
    n = 2 * STAGES
    out_shape = (
        jax.ShapeDtypeStruct((1, RANK, dim), bf16),
        jax.ShapeDtypeStruct((1, RANK, features), f32),
        jax.ShapeDtypeStruct((1, RANK, features), bf16),
        jax.ShapeDtypeStruct((1, RANK, dim), f32),
    )
    scratch = [
        pltpu.VMEM(norm_in.shape, bf16),
        pltpu.VMEM(query_grad.shape, bf16),
        pltpu.VMEM(attn_out.shape, bf16),
        pltpu.VMEM(sketch_q.shape, bf16),
        pltpu.VMEM(sketch_o.shape, bf16),
        pltpu.VMEM((1, tokens, dim), bf16),
        pltpu.VMEM((n, NY, RANK, 128), bf16),
        pltpu.VMEM((n, NY, RANK, 128), bf16),
        pltpu.VMEM((2, NY, 8, 128), f32),
        pltpu.VMEM((2, GROUP, 8, 128), f32),
        pltpu.VMEM((2, RANK, 128), f32),
        pltpu.VMEM((STAGES, GROUP, RANK, wide), bf16),
        pltpu.VMEM((STAGES, GROUP, RANK, narrow), bf16),
        pltpu.VMEM((STAGES, GROUP, RANK, wide), bf16),
        pltpu.VMEM((STAGES, GROUP, RANK, narrow), bf16),
        pltpu.VMEM((STAGES, 2, RANK, wide), bf16),
        pltpu.VMEM((STAGES, 2, RANK, narrow), bf16),
        pltpu.VMEM((STAGES, GROUP, RANK, wide), bf16),
        pltpu.VMEM((STAGES, GROUP, RANK, narrow), bf16),
        dma((2,)),
        dma((n, NY - 1)),
        dma((n, NY - 1)),
        dma((n, NY - 1)),
        dma((n, NY - 1)),
        dma((n, GROUP - 1)),
        dma((n, GROUP - 1)),
        dma((n,)),
        dma((n,)),
        dma((n, GROUP - 1)),
        dma((n, GROUP - 1)),
        dma((2, NY - 1)),
        dma((2, NY - 1)),
        dma((2, GROUP - 1)),
        dma((2, GROUP - 1)),
        dma((5,)),
    ]
    return pl.pallas_call(
        kernel,
        out_shape=out_shape,
        in_specs=[pl.BlockSpec(memory_space=pltpu.HBM)] * 6,
        out_specs=(vmem,) * 4,
        scratch_shapes=scratch,
        compiler_params=pltpu.CompilerParams(
            collective_id=0, has_side_effects=True, vmem_limit_bytes=65800000
        ),
        name="adapters",
    )(*operands)


def solution(mesh):
    row = P("section", "dp", "tensor")
    thin = P("section", None, "tensor")
    return jax.shard_map(
        body,
        mesh=mesh,
        in_specs=(row, row, row, row, thin, thin),
        out_specs=(thin, thin, thin, thin),
        check_vma=False,
    )
```

time: 190 us -> 178 us (0.937)
  Pallas kernels: 184 us -> 173 us
    pallas_call x1, Pallas kernels: 184 us -> 173 us  [body(): pl.pallas_call(kernel, out_shape=out_shape, in_specs=[pl.BlockSpec(memory...]
where the time goes in v3:
time: 178 us
  Pallas kernels  173 us (97%)
  local copies, waits for them, and re-layouts  4.19 us (2%)
    pallas_call x1, Pallas kernels, body(): pl.pallas_call(kernel, out_shape=out_shape, in_specs=[pl.BlockSpec(memory...  173 us
    unnamed x10, local copies, waits for them, and re-layouts  4.19 us

profile of v3, /device:TPU:1, one launch (start us, length us, event | category | flops | bytes accessed | tf_op | source)
XLA Modules:
  0.0 178.0 jit_solution(3804007361223996693)
XLA Ops:
  0.6 173.2 %adapters.1 = (bf16[1,64,2048]{2,1,0:T(8,128)(2,1)}, f32[1,64,1024]{2,1,0:T(8,128)}, bf16[1,64,1024]{2,1,0:T(8,128)(2,1)}, f32[1,64,2048]{2,1,0:T(8,128)}) custom-call(bf16[1,128,2048]{2,1,0:T(8,128)(2,1)} %norm_hbm.1, bf16[1,128,1024]{2,1,0:T(8,128)(2,1)} %query_hbm.1, bf16[1,128,1024]{2,1,0:T(8,128)(2,1)} %attn_hbm.1, bf16[1,128,2048]{2,1,0:T(8,128)(2,1)} %handed_hbm.1, ...), custom_call_target="tpu_custom_call" | custom-call | tf_op jit(solution)/shard_map/adapters/pallas_call | solution.py:342
  173.8 0.0 copy-start.1
  173.8 0.0 copy-start
  173.8 1.7 copy.14
  175.6 0.0 copy-done.1
  175.6 0.0 copy-start.2
  175.6 0.7 copy.15
  176.3 0.3 copy-done.2
  176.6 0.7 copy.16
  177.2 0.0 copy-done
  177.2 0.8 copy.17
Async XLA Ops:
  173.8 1.8 copy-start.1
  173.8 3.4 %copy-start = (f32[1,64,2048]{2,1,0:T(8,128)S(1)}, f32[1,64,2048]{2,1,0:T(8,128)}, u32[]{:S(2)}) copy-start(f32[1,64,2048]{2,1,0:T(8,128)} %get-tuple-element.11) | copy-start | bytes 1572868
  175.6 1.0 copy-start.2

commit v4 on v3

--- a/solution.py
+++ b/solution.py
@@ -12,6 +12,8 @@
 STAGES = 2 * POWER + 2
 NY = 4
 GROUP = 8
+FAR = (4, 3, 5, 2, 6, 1, 7)
+FAR_Y = (2, 1, 3)
 MESH = pl.DeviceIdType.MESH
 ORDER = [
     0, 0, 0, 2, 1, 1, 1, 0, 1, 0, 1, 0, 1, 0, 0, 1, 1, 0, 1, 0, 0, 1, 0, 1,
@@ -126,17 +128,17 @@
                 part = dot_rows(sketch[0], before[0])
             else:
                 part = None
-                for r in range(GROUP):
+                for r in (0,) + FAR[::-1]:
                     source = (me + GROUP - r) % GROUP
                     if r > 0:
-                        gathers[r - 1].wait_recv()
+                        gathers[FAR.index(r)].wait_recv()
                     columns = pl.ds(pl.multiple_of(source * width, 128), width)
                     term = dot_rows(last[source], before[0, :, columns])
                     part = term if part is None else part + term
             y_buf[idx, y] = part.astype(bf16)
             ready()
             own = y_buf.at[idx, y]
-            factors = [remote(own, own, y_send.at[idx, r - 1], y_recv.at[idx, r - 1], y_peer(r)) for r in range(1, NY)]
+            factors = [remote(own, own, y_send.at[idx, r - 1], y_recv.at[idx, r - 1], y_peer(r)) for r in FAR_Y]
             pending.extend(factors)
             if k > 0:
                 gram = None
@@ -161,7 +163,7 @@
                 token_sum = token_sum + y_buf[idx, j].astype(f32)
             rows = token_sum.astype(bf16)
             scatters = []
-            for r in range(1, GROUP + 1):
+            for r in FAR + (GROUP,):
                 other = (me + r) % GROUP
                 columns = pl.ds(pl.multiple_of(other * wide, 128), wide)
                 piece = jnp.dot(rows, here[0, :, columns], preferred_element_type=f32).astype(bf16)
@@ -223,7 +225,7 @@
             own = everyone.at[me]
             gathers = [
                 remote(own, own, ag_send.at[idx, r - 1], ag_recv.at[idx, r - 1], group_peer(r))
-                for r in range(1, GROUP)
+                for r in FAR
             ]
             pending.extend(gathers)
             last = everyone

time: 178 us -> 176 us (0.989)
  Pallas kernels: 173 us -> 171 us
    pallas_call x1, Pallas kernels: 173 us -> 171 us  [body(): pl.pallas_call(kernel, out_shape=out_shape, in_specs=[pl.BlockSpec(memory...]
where the time goes in v4:
time: 176 us; the launch traced here: 175 us
  Pallas kernels  171 us (97%)
  local copies, waits for them, and re-layouts  4.19 us (2%)
    pallas_call x1, Pallas kernels, body(): pl.pallas_call(kernel, out_shape=out_shape, in_specs=[pl.BlockSpec(memory...  171 us
    unnamed x10, local copies, waits for them, and re-layouts  4.19 us

profile of v4, /device:TPU:1, one launch (start us, length us, event | category | flops | bytes accessed | tf_op | source)
XLA Modules:
  0.0 175.5 jit_solution(9865996734202203171)
XLA Ops:
  0.6 170.6 %adapters.1 = (bf16[1,64,2048]{2,1,0:T(8,128)(2,1)}, f32[1,64,1024]{2,1,0:T(8,128)}, bf16[1,64,1024]{2,1,0:T(8,128)(2,1)}, f32[1,64,2048]{2,1,0:T(8,128)}) custom-call(bf16[1,128,2048]{2,1,0:T(8,128)(2,1)} %norm_hbm.1, bf16[1,128,1024]{2,1,0:T(8,128)(2,1)} %query_hbm.1, bf16[1,128,1024]{2,1,0:T(8,128)(2,1)} %attn_hbm.1, bf16[1,128,2048]{2,1,0:T(8,128)(2,1)} %handed_hbm.1, ...), custom_call_target="tpu_custom_call" | custom-call | tf_op jit(solution)/shard_map/adapters/pallas_call | solution.py:344
  171.3 0.0 copy-start.1
  171.3 0.0 copy-start
  171.3 1.7 copy.14
  173.0 0.0 copy-done.1
  173.0 0.0 copy-start.2
  173.0 0.7 copy.15
  173.7 0.3 copy-done.2
  174.0 0.7 copy.16
  174.7 0.0 copy-done
  174.7 0.8 copy.17
Async XLA Ops:
  171.3 1.8 %copy-start.1 = (f32[1,64,1024]{2,1,0:T(8,128)S(1)}, f32[1,64,1024]{2,1,0:T(8,128)}, u32[]{:S(2)}) copy-start(f32[1,64,1024]{2,1,0:T(8,128)} %get-tuple-element.9) | copy-start | bytes 786436
  171.3 3.4 %copy-start = (f32[1,64,2048]{2,1,0:T(8,128)S(1)}, f32[1,64,2048]{2,1,0:T(8,128)}, u32[]{:S(2)}) copy-start(f32[1,64,2048]{2,1,0:T(8,128)} %get-tuple-element.11) | copy-start | bytes 1572868
  173.0 1.0 copy-start.2
